TPU v7x, 32 devices: a whole 2x2x4 slice. The times are simulated.
32 devices in a mesh: row: 8 (over z, core), col: 4 (over y, x).
Axes of the slice: x: 2, y: 2, z: 4, core: 2. Of those that a mesh axis runs over, the one named last changes fastest.
Arguments:
- covariance: float32 [8192, 8192], P('row', 'col'), as said below
- state_mean: float32 [8192], P('row'), may hold values from -6 to 6
- obs_values: float32 [2, 256], replicated, may hold values from -8 to 8
- obs_cells: int32 [2, 4, 256], replicated, may hold values from 0 to 8191
- obs_weights: float32 [2, 4, 256], replicated, may hold values from 0.2 to 1
- obs_variance: float32 [2, 256], replicated, may hold values from 0.05 to 1
Outputs:
- covariance_after: float32 [8192, 8192], P('row', 'col')
- state_after: float32 [8192], P('row')
Inputs may be any that keep to these rules, and one draw needn't show every extreme that they name: `covariance`: symmetric and positive definite.
All inputs are finite; a program needn't handle non-finite values.
Results may differ from a plain program's by a relative error of at most 0.0001.
Values sent between devices are 32-bit elements; how exact they have to be, the bound alone decides.
A program may use at most 64 MiB of HBM per device.

v0:
```python
import functools

import jax
import jax.numpy as jnp
from jax import lax
from jax.experimental import pallas as pl
from jax.experimental.pallas import tpu as pltpu
from jax.sharding import PartitionSpec as P

HI = lax.Precision.HIGHEST
MID = lax.Precision.HIGH
MESH = pl.DeviceIdType.MESH
BLK = 128
SUB = 8

def base_inverse(work, cols, midway):
    def panel_step(g, carry):
        start = pl.multiple_of(g * SUB, SUB)
        panel = work[pl.ds(start, SUB), :]
        cols[:, :SUB] = panel[:, :BLK].T
        square = cols[pl.ds(start, SUB), :SUB]
        wide = [jnp.broadcast_to(square[:, j : j + 1], (SUB, BLK)) for j in range(SUB)]
        left, right = panel[:, :BLK], panel[:, BLK:]
        below = lax.broadcasted_iota(jnp.int32, (SUB, BLK), 0)
        scale = jnp.zeros((SUB, BLK), jnp.float32)
        for j in range(SUB):
            pivot = jnp.broadcast_to(wide[j][j : j + 1, :], (SUB, BLK))
            inv = 1.0 / pivot
            scale = jnp.where(below == j, lax.rsqrt(pivot), scale)
            ratio = jnp.where(below > j, wide[j] * inv, 0.0)
            left = left - ratio * left[j : j + 1, :]
            right = right - ratio * right[j : j + 1, :]
            for k in range(j + 1, SUB):
                wide[k] = wide[k] - ratio * wide[k][j : j + 1, :]
        left = left * scale
        right = right * scale
        both = jnp.concatenate([left, right], axis=1)
        lane = lax.broadcasted_iota(jnp.int32, (SUB, BLK), 1)
        lhs = jnp.where(lane >= start + SUB, left, 0.0)
        work[pl.ds(start, SUB), :] = both
        work[...] = work[...] - lax.dot_general(lhs, both, (((0,), (0,)), ((), ())), precision=HI, preferred_element_type=jnp.float32)
        return carry
    half = BLK // SUB // 2
    lax.fori_loop(0, half, panel_step, 0)
    midway()
    lax.fori_loop(half, 2 * half, panel_step, 0)

def factor_inverse(mat, work, cols, between):
    size = mat.shape[0]
    eye = (lax.broadcasted_iota(jnp.int32, (BLK, BLK), 0) == lax.broadcasted_iota(jnp.int32, (BLK, BLK), 1)).astype(jnp.float32)
    for b in range(size // BLK):
        lo, hi = b * BLK, (b + 1) * BLK
        work[:, :BLK] = mat[lo:hi, lo:hi]
        work[:, BLK:] = eye
        base_inverse(work, cols, lambda: between(2 * b))
        winv = work[:, BLK:]
        if hi < size:
            panel = jnp.dot(winv, mat[lo:hi, hi:size], precision=HI, preferred_element_type=jnp.float32)
        if lo > 0:
            left = jnp.dot(winv, mat[lo:hi, size : size + lo], precision=HI, preferred_element_type=jnp.float32)
            mat[lo:hi, size : size + lo] = left
        mat[lo:hi, size + lo : size + hi] = winv
        if hi < size:
            right = mat[lo:hi, size : size + hi]
            dims = (((0,), (0,)), ((), ()))
            mat[hi:size, hi:size] = mat[hi:size, hi:size] - lax.dot_general(panel, panel, dims, precision=HI, preferred_element_type=jnp.float32)
            mat[hi:size, size : size + hi] = mat[hi:size, size : size + hi] - lax.dot_general(panel, right, dims, precision=HI, preferred_element_type=jnp.float32)
        between(2 * b + 1)


def pair_blocks(size):
    count = size // BLK
    return [(i, j) for i in range(count) for j in range(i + 1)]


def kernel(
    nr, nc, t_ref, op_ref, part_ref, var_ref, inv_ref, xr_ref, xc_ref, pred_ref,
    acc, full, land, tland, mat, work, cols, send_sem, recv_sem,
):
    ratio = nr // nc
    row, col = lax.axis_index("row"), lax.axis_index("col")
    high, low = row // ratio, row % ratio
    packed = acc.shape[0]
    rows, size = t_ref.shape
    chunk = rows // nc
    sub = chunk // 2
    pieces = 2 * nc
    used = [0]

    def take(count):
        used[0] += count
        return used[0] - count

    levels = [
        (ratio, low, lambda d: (high * ratio + lax.rem(low + d, ratio), col)),
        (nc, col, lambda d: (row, lax.rem(col + d, nc))),
        (nc, high, lambda d: (lax.rem(high + d, nc) * ratio + low, col)),
    ]
    barrier = pltpu.get_barrier_semaphore()
    for n, me, peer in levels:
        for d in range(1, n):
            pl.semaphore_signal(barrier, inc=1, device_id=peer(d), device_id_type=MESH)
    pl.semaphore_wait(barrier, ratio - 1 + 2 * (nc - 1))

    def remote(src, dst, sem, device):
        return pltpu.make_async_remote_copy(
            src_ref=src, dst_ref=dst, send_sem=send_sem.at[sem], recv_sem=recv_sem.at[sem],
            device_id=device, device_id_type=MESH,
        )

    t_base = take(2 * (nc - 1))
    _, _, col_peer = levels[1]
    t_copies = []
    for h in range(2):
        for d in range(1, nc):
            other = lax.rem(col + d, nc)
            src = t_ref.at[pl.ds(pl.multiple_of(other * chunk + h * sub, 8), sub)]
            dst = tland.at[d - 1, pl.ds(h * sub, sub)]
            t_copies.append(remote(src, dst, t_base + h * (nc - 1) + d - 1, col_peer(d)))
    for copy in t_copies[: nc - 1]:
        copy.start()

    place = 0
    for i in range(size // BLK):
        block = lax.dot_general(
            op_ref[:, i * BLK : (i + 1) * BLK], t_ref[:, : (i + 1) * BLK], (((0,), (0,)), ((), ())),
            precision=MID, preferred_element_type=jnp.float32,
        )
        for j in range(i + 1):
            acc[place : place + BLK, :] = block[:, j * BLK : (j + 1) * BLK]
            place += BLK
    acc[place : place + 8, :] = part_ref[...]
    acc[place + 8 :, :] = jnp.zeros((packed - place - 8, BLK), jnp.float32)
    start, length, slot = 0, packed, 0
    spots = []
    for level, (n, me, peer) in enumerate(levels):
        part = length // n
        base = take(n - 1)
        copies = []
        for d in range(1, n):
            other = lax.rem(me + d, n)
            src = acc.at[pl.ds(pl.multiple_of(start + other * part, 8), part)]
            dst = land.at[pl.ds(slot + (d - 1) * part, part)]
            copies.append(remote(src, dst, base + d - 1, peer(d)))
            copies[-1].start()
        if level == 1:
            for copy in t_copies[nc - 1 :]:
                copy.start()
        start = pl.multiple_of(start + me * part, 8)
        length = part
        spots.append((start, part))
        for copy in copies:
            copy.wait()
        mine = acc[pl.ds(start, part), :]
        for d in range(1, n):
            mine = mine + land[pl.ds(slot + (d - 1) * part, part), :]
        acc[pl.ds(start, part), :] = mine
        slot += (n - 1) * part
    full[pl.ds(start, length), :] = acc[pl.ds(start, length), :]

    for level in (2, 1, 0):
        n, me, peer = levels[level]
        begin, part = spots[level]
        base = take(n - 1)
        copies = []
        for d in range(1, n):
            where = full.at[pl.ds(begin, part)]
            copies.append(remote(where, where, base + d - 1, peer(d)))
            copies[-1].start()
        for copy in copies:
            copy.wait()

    gather_base = take(2 * (nc - 1))
    chain_base = take(pieces)
    down_base = take(pieces)
    sib_base = take(pieces * (ratio - 1))
    gathers = []
    for d in range(1, nc):
        for h in range(2):
            own = xr_ref.at[pl.ds(pl.multiple_of(col * chunk + h * sub, 8), sub)]
            gathers.append(remote(own, own, gather_base + 2 * (d - 1) + h, col_peer(d)))
    _, _, low_peer = levels[0]
    source = high == col
    top = nc - 1
    above = (jnp.minimum(high + 1, top) * ratio + low, col)
    below = (jnp.maximum(high - 1, 0) * ratio + low, col)
    goes_up = jnp.logical_and(high >= col, high < top)
    goes_down = jnp.logical_and(high <= col, high > 0)
    onward = jnp.logical_or(goes_up, goes_down)
    middle = jnp.logical_and(onward, jnp.logical_not(source))
    last = jnp.logical_and(jnp.logical_not(onward), jnp.logical_not(source))

    def links(e, src_is_own):
        begin = pl.multiple_of(lax.rem(col - e // 2 + nc, nc) * chunk + (e % 2) * sub, 8)
        dst = xc_ref.at[low, pl.ds(begin, sub)]
        src = xr_ref.at[pl.ds(begin, sub)] if src_is_own else dst
        up = remote(src, dst, chain_base + e, above)
        down = pltpu.make_async_remote_copy(
            src_ref=src, dst_ref=dst, send_sem=send_sem.at[down_base + e],
            recv_sem=recv_sem.at[chain_base + e], device_id=below, device_id_type=MESH,
        )
        sibs = [remote(src, dst, sib_base + e * (ratio - 1) + q - 1, low_peer(q)) for q in range(1, ratio)]
        return begin, up, down, sibs

    def send_on(up, down, sibs):
        @pl.when(goes_up)
        def _():
            up.start()

        @pl.when(goes_down)
        def _():
            down.start()

        for sib in sibs:
            sib.start()

    def relay_source(e):
        if e >= 2:
            gathers[e - 2].wait_recv()
        begin, up, down, sibs = links(e, True)
        send_on(up, down, sibs)
        xc_ref[low, pl.ds(begin, sub), :] = xr_ref[pl.ds(begin, sub), :]

    def relay_middle(e):
        begin, up, down, sibs = links(e, False)
        up.wait_recv()
        send_on(up, down, sibs)

    def relay_last(e):
        begin, up, down, sibs = links(e, False)
        up.wait_recv()
        for sib in sibs:
            sib.start()

    def between(event):
        @pl.when(source)
        def _():
            if 2 <= event + 1 < pieces:
                relay_source(event + 1)

        @pl.when(middle)
        def _():
            if event < pieces:
                relay_middle(event)

        @pl.when(last)
        def _():
            if 0 <= event - 2 < pieces:
                relay_last(event - 2)

    for copy in t_copies:
        copy.wait()
    where = pl.ds(pl.multiple_of(col * chunk, 8), chunk)
    owned = t_ref[where, :]
    for d in range(1, nc):
        owned = owned + tland[d - 1]
    xr_ref[where, :] = owned

    @pl.when(source)
    def _():
        relay_source(0)
        relay_source(1)

    for copy in gathers:
        copy.start()

    same = lax.broadcasted_iota(jnp.int32, (BLK, BLK), 0) == lax.broadcasted_iota(jnp.int32, (BLK, BLK), 1)
    for index, (i, j) in enumerate(pair_blocks(size)):
        block = full[index * BLK : (index + 1) * BLK, :]
        if i == j:
            block = 0.5 * (block + block.T) + jnp.where(same, var_ref[:, i * BLK : (i + 1) * BLK], 0.0)
        mat[i * BLK : (i + 1) * BLK, j * BLK : (j + 1) * BLK] = block
        if i != j:
            mat[j * BLK : (j + 1) * BLK, i * BLK : (i + 1) * BLK] = block.T
    mat[:, size:] = jnp.zeros((size, size), jnp.float32)
    tail = len(pair_blocks(size)) * BLK
    pred_ref[...] = full[tail : tail + 8, :]

    events = 2 * (size // BLK)
    factor_inverse(mat, work, cols, between)
    inv_ref[...] = mat[:, size:]
    for event in range(events, pieces + 2):
        between(event)
    for copy in gathers:
        copy.wait_send()

    @pl.when(jnp.logical_not(source))
    def _():
        for copy in gathers:
            copy.wait_recv()

    for e in range(pieces):
        _, up, down, sibs = links(e, False)

        @pl.when(goes_up)
        def _():
            up.wait_send()

        @pl.when(goes_down)
        def _():
            down.wait_send()

        for sib in sibs:
            sib.wait()


def exchange(mesh, total, part, row_op, part_pred, variance):
    nr, nc = mesh.shape["row"], mesh.shape["col"]
    ratio = nr // nc
    rows, size = part.shape
    landing, length = 0, total
    for n in (ratio, nc, nc):
        landing += (n - 1) * (length // n)
        length //= n
    sems = 2 * (ratio - 1 + 2 * (nc - 1)) + 4 * (nc - 1) + 4 * nc + 2 * nc * (ratio - 1)
    f32 = jnp.float32
    vmem = pl.BlockSpec(memory_space=pltpu.VMEM)
    return pl.pallas_call(
        functools.partial(kernel, nr, nc),
        out_shape=(
            jax.ShapeDtypeStruct((size, size), f32),
            jax.ShapeDtypeStruct((rows, size), f32),
            jax.ShapeDtypeStruct((ratio, rows, size), f32),
            jax.ShapeDtypeStruct((8, BLK), f32),
        ),
        in_specs=[vmem] * 4,
        out_specs=(vmem,) * 4,
        scratch_shapes=[
            pltpu.VMEM((total, BLK), f32),
            pltpu.VMEM((total, BLK), f32),
            pltpu.VMEM((landing, BLK), f32),
            pltpu.VMEM((nc - 1, rows // nc, size), f32),
            pltpu.VMEM((size, 2 * size), f32),
            pltpu.VMEM((BLK, 2 * BLK), f32),
            pltpu.VMEM((BLK, BLK), f32),
            pltpu.SemaphoreType.DMA((sems,)),
            pltpu.SemaphoreType.DMA((sems,)),
        ],
        compiler_params=pltpu.CompilerParams(collective_id=0, has_side_effects=True, vmem_limit_bytes=40 * 1024 * 1024),
    )(part, row_op, part_pred, variance)


def dot(a, b, precision):
    return jnp.dot(a, b, precision=precision, preferred_element_type=jnp.float32)


def local_operator(cells, weights, start, count):
    positions = start + lax.iota(jnp.int32, count)[:, None]
    total = jnp.zeros((count, cells.shape[1]), jnp.float32)
    for foot in range(cells.shape[0]):
        total = total + jnp.where(cells[foot][None, :] == positions, weights[foot][None, :], 0.0)
    return total


def on_device(mesh, covariance, state_mean, obs_values, obs_cells, obs_weights, obs_variance):
    rows_dev, cols_dev = covariance.shape
    row_index = lax.axis_index("row")
    col_index = lax.axis_index("col")
    devices = mesh.shape["row"] * mesh.shape["col"]
    batches, foot, width = obs_cells.shape
    total = batches * width
    cells = obs_cells.transpose(1, 0, 2).reshape(foot, total)
    weights = obs_weights.transpose(1, 0, 2).reshape(foot, total)
    values = obs_values.reshape(total)
    variance = obs_variance.reshape(1, total)
    col_op = local_operator(cells, weights, col_index * cols_dev, cols_dev)
    row_op = local_operator(cells, weights, row_index * rows_dev, rows_dev)
    part = dot(covariance, col_op, MID)
    part_pred = jnp.sum(row_op * state_mean[:, None], axis=0)
    part_pred = jnp.where(col_index == 0, part_pred, 0.0).reshape(total // BLK, BLK)
    part_pred = jnp.pad(part_pred, ((0, 8 - total // BLK), (0, 0)))
    filled = len(pair_blocks(total)) * BLK + 8
    unit = 8 * devices
    packed = -(-(filled + 8) // unit) * unit
    inverse, cross, cross_cols, pred = exchange(mesh, packed, part, row_op, part_pred, variance)
    predicted = pred[: total // BLK].reshape(total)
    innov = values - predicted
    white = dot(inverse, innov[:, None], HI)
    gain = dot(cross, inverse.T, MID)
    gain_cols = dot(cross_cols.reshape(cols_dev, total), inverse.T, MID)
    mean = state_mean + dot(gain, white, HI)[:, 0]
    matrix = covariance - dot(gain, gain_cols.T, MID)
    return (matrix, mean)


def solution(mesh):
    return jax.shard_map(
        functools.partial(on_device, mesh),
        mesh=mesh,
        in_specs=(P("row", "col"), P("row"), P(), P(), P(), P()),
        out_specs=(P("row", "col"), P("row")),
        check_vma=False,
    )
```

profile of v0, /device:TPU:7, one launch (start us, length us, event | category | flops | bytes accessed | tf_op | source)
XLA Modules:
  0.0 137.5 jit_solution(11309831550106075565)
XLA Ops:
  0.6 0.7 copy.11
  1.3 0.7 copy.10
  2.0 0.9 fusion.26
  2.9 0.9 fusion.27
  3.7 0.0 copy-start
  3.7 10.7 %fusion.22.t_ref = f32[1024,512]{1,0:T(8,128)S(1)} fusion(f32[1024,2048]{1,0:T(8,128)} %param.6, f32[512]{0:T(512)S(1)} %bitcast.54, s32[512]{0:T(512)S(1)} %bitcast.46, f32[512]{0:T(512)S(1)} %bitcast.56, s32[512]{0:T(512)S(1)} %bitcast.48, f32[512]{0:T(512)S(1)} %bitcast.58, s32[512]{0:T(512)S(1)} %bitcast.50, f32[512]{0:T(512)S(1)} %bitcast.52, ...), kind=kOutput, calls=%fused_computation.25 | convolution fusion | flops 6453985280 | bytes 10510336 | tf_op jit(solution)/shard_map/dot_general | solution.py:344
  14.4 0.0 copy-done
  14.4 1.0 multiply_reduce_fusion
  15.4 103.6 %shard_map.77 = (f32[512,512]{1,0:T(8,128)S(1)}, f32[1024,512]{1,0:T(8,128)S(1)}, f32[2,1024,512]{2,1,0:T(8,128)S(1)}, f32[8,128]{1,0:T(8,128)S(1)}) custom-call(f32[1024,512]{1,0:T(8,128)S(1)} %fusion.22.t_ref, f32[1024,512]{1,0:T(8,128)S(1)} %get-tuple-element.11.op_ref, f32[8,128]{1,0:T(8,128)S(1)} %pad.4.part_ref, f32[1,512]{1,0:T(1,128)S(1)} %bitcast.39), custom_call_target="tpu_custom_call" | custom-call | tf_op jit(solution)/shard_map/pallas_call | solution.py:318
  119.0 1.0 convolution_bitcast_fusion
  120.0 0.0 slice-start
  120.0 1.9 %fusion.28 = f32[1024,512]{1,0:T(8,128)S(1)} fusion(f32[1024,512]{1,0:T(8,128)S(1)} %get-tuple-element.6, f32[512,512]{1,0:T(8,128)S(1)} %get-tuple-element.7), kind=kOutput, calls=%fused_computation.34 | convolution fusion | flops 1610612736 | bytes 5242880 | tf_op jit(solution)/shard_map/dot_general | solution.py:344
  121.9 0.0 slice-start.1
  121.9 3.7 %fusion.29 = f32[2048,512]{1,0:T(8,128)S(1)} fusion(f32[2048,512]{1,0:T(8,128)S(1)} %bitcast.38, f32[512,512]{1,0:T(8,128)S(1)} %get-tuple-element.7), kind=kOutput, calls=%fused_computation.35 | convolution fusion | flops 3221225472 | bytes 9437184 | tf_op jit(solution)/shard_map/dot_general | solution.py:344
  125.6 1.9 %fusion.30 = f32[1,1024]{1,0:T(1,128)S(1)} fusion(f32[1024,512]{1,0:T(8,128)S(1)} %fusion.28, f32[512,1]{0,1:T(1,128)S(1)} %convolution_bitcast_fusion), kind=kOutput, calls=%fused_computation.36 | convolution fusion | flops 6291456 | bytes 2103296 | tf_op jit(solution)/shard_map/dot_general | solution.py:344
  127.5 0.6 add.55
  128.1 0.0 slice-done
  128.1 0.0 slice-done.1
  128.1 9.4 %convolution_subtract_fusion = f32[1024,2048]{1,0:T(8,128)} fusion(f32[1024,2048]{1,0:T(8,128)S(1)} %bitcast.41, f32[1024,512]{1,0:T(8,128)S(1)} %fusion.28, f32[2048,512]{1,0:T(8,128)S(1)} %fusion.29), kind=kOutput, calls=%fused_computation.12 | convolution fusion | flops 6444548096 | bytes 23068672 | tf_op jit(solution)/shard_map/dot_general | solution.py:344
  (6 shorter events, 0.0 us)
Async XLA Ops:
  3.7 10.7 %copy-start = (f32[1024]{0:T(1024)S(1)}, f32[1024]{0:T(1024)}, u32[]{:S(2)}) copy-start(f32[1024]{0:T(1024)} %param.7) | copy-start | bytes 12292
  120.0 8.1 %slice-start = ((s8[8388608]{0:T(1024)(128)(4,1)}), s8[4194304]{0:T(1024)(128)(4,1)S(1)}, s32[]{:S(2)}) async-start(s8[8388608]{0:T(1024)(128)(4,1)} %bitcast.40), calls=%async_computation | async-start | bytes 8388608
  121.9 6.2 %slice-start.1 = ((s8[8388608]{0:T(1024)(128)(4,1)}), s8[4194304]{0:T(1024)(128)(4,1)S(1)}, s32[]{:S(2)}) async-start(s8[8388608]{0:T(1024)(128)(4,1)} %bitcast.40), calls=%async_computation.1 | async-start | bytes 8388608
where the time goes:
time: 138 us
  Pallas kernels  104 us (75%)
  matrix products  28.5 us (21%)
  local copies, waits for them, and re-layouts  3.1 us (2%)
  other arithmetic  1.6 us (1%)
    pallas_call x1, Pallas kernels, exchange(): pl.pallas_call(functools.partial(kernel, nr, nc), out_shape=(jax.ShapeDty...  104 us
    dot_general x6, matrix products, dot(): jnp.dot(a, b, precision=precision, preferred_element_type=jnp.float32)  28.5 us

commit v1 on v0

--- a/solution.py
+++ b/solution.py
@@ -14,7 +14,7 @@
 SUB = 8
 
 def base_inverse(work, cols, midway):
-    def panel_step(g, carry):
+    def panel_step(first, g, carry):
         start = pl.multiple_of(g * SUB, SUB)
         panel = work[pl.ds(start, SUB), :]
         cols[:, :SUB] = panel[:, :BLK].T
@@ -38,12 +38,14 @@
         lane = lax.broadcasted_iota(jnp.int32, (SUB, BLK), 1)
         lhs = jnp.where(lane >= start + SUB, left, 0.0)
         work[pl.ds(start, SUB), :] = both
-        work[...] = work[...] - lax.dot_general(lhs, both, (((0,), (0,)), ((), ())), precision=HI, preferred_element_type=jnp.float32)
+        work[first:, :] = work[first:, :] - lax.dot_general(lhs[:, first:], both, (((0,), (0,)), ((), ())), precision=HI, preferred_element_type=jnp.float32)
         return carry
-    half = BLK // SUB // 2
-    lax.fori_loop(0, half, panel_step, 0)
-    midway()
-    lax.fori_loop(half, 2 * half, panel_step, 0)
+    steps = BLK // SUB // 4
+    for quarter in range(4):
+        if quarter == 2:
+            midway()
+        first = quarter * steps * SUB
+        lax.fori_loop(quarter * steps, (quarter + 1) * steps, functools.partial(panel_step, first), 0)
 
 def factor_inverse(mat, work, cols, between):
     size = mat.shape[0]
@@ -52,7 +54,7 @@
         lo, hi = b * BLK, (b + 1) * BLK
         work[:, :BLK] = mat[lo:hi, lo:hi]
         work[:, BLK:] = eye
-        base_inverse(work, cols, lambda: between(2 * b))
+        base_inverse(work, cols, lambda: between(2 * b + 1))
         winv = work[:, BLK:]
         if hi < size:
             panel = jnp.dot(winv, mat[lo:hi, hi:size], precision=HI, preferred_element_type=jnp.float32)
@@ -65,7 +67,7 @@
             dims = (((0,), (0,)), ((), ()))
             mat[hi:size, hi:size] = mat[hi:size, hi:size] - lax.dot_general(panel, panel, dims, precision=HI, preferred_element_type=jnp.float32)
             mat[hi:size, size : size + hi] = mat[hi:size, size : size + hi] - lax.dot_general(panel, right, dims, precision=HI, preferred_element_type=jnp.float32)
-        between(2 * b + 1)
+        between(2 * b + 2)
 
 
 def pair_blocks(size):
@@ -74,8 +76,8 @@
 
 
 def kernel(
-    nr, nc, t_ref, op_ref, part_ref, var_ref, inv_ref, xr_ref, xc_ref, pred_ref,
-    acc, full, land, tland, mat, work, cols, send_sem, recv_sem,
+    nr, nc, t_ref, op_ref, part_ref, var_ref, inv_ref, gain_ref, xc_ref, pred_ref,
+    xr_ref, acc, full, land, tland, mat, work, cols, send_sem, recv_sem,
 ):
     ratio = nr // nc
     row, col = lax.axis_index("row"), lax.axis_index("col")
@@ -119,6 +121,108 @@
             t_copies.append(remote(src, dst, t_base + h * (nc - 1) + d - 1, col_peer(d)))
     for copy in t_copies[: nc - 1]:
         copy.start()
+
+    gather_base = take(2 * (nc - 1))
+    chain_base = take(pieces)
+    down_base = take(pieces)
+    sib_base = take(pieces * (ratio - 1))
+    gathers = []
+    for h in range(2):
+        for d in range(1, nc):
+            own = xr_ref.at[pl.ds(pl.multiple_of(col * chunk + h * sub, 8), sub)]
+            gathers.append(remote(own, own, gather_base + h * (nc - 1) + d - 1, col_peer(d)))
+    _, _, low_peer = levels[0]
+    source = high == col
+    top = nc - 1
+    above = (jnp.minimum(high + 1, top) * ratio + low, col)
+    below = (jnp.maximum(high - 1, 0) * ratio + low, col)
+    goes_up = jnp.logical_and(high >= col, high < top)
+    goes_down = jnp.logical_and(high <= col, high > 0)
+    onward = jnp.logical_or(goes_up, goes_down)
+    middle = jnp.logical_and(onward, jnp.logical_not(source))
+    last = jnp.logical_and(jnp.logical_not(onward), jnp.logical_not(source))
+
+    spot = [(0, 0), (0, 1)] + [(d, h) for h in range(2) for d in range(1, nc)]
+
+    def links(e, src_is_own):
+        begin = pl.multiple_of(lax.rem(col - spot[e][0] + nc, nc) * chunk + spot[e][1] * sub, 8)
+        dst = xc_ref.at[low, pl.ds(begin, sub)]
+        src = xr_ref.at[pl.ds(begin, sub)] if src_is_own else dst
+        up = remote(src, dst, chain_base + e, above)
+        down = pltpu.make_async_remote_copy(
+            src_ref=src, dst_ref=dst, send_sem=send_sem.at[down_base + e],
+            recv_sem=recv_sem.at[chain_base + e], device_id=below, device_id_type=MESH,
+        )
+        sibs = [remote(src, dst, sib_base + e * (ratio - 1) + q - 1, low_peer(q)) for q in range(1, ratio)]
+        return begin, up, down, sibs
+
+    def send_on(up, down, sibs):
+        @pl.when(goes_up)
+        def _():
+            up.start()
+
+        @pl.when(goes_down)
+        def _():
+            down.start()
+
+        for sib in sibs:
+            sib.start()
+
+    def relay_source(e):
+        if e >= 2:
+            gathers[e - 2].wait_recv()
+        begin, up, down, sibs = links(e, True)
+        send_on(up, down, sibs)
+        xc_ref[low, pl.ds(begin, sub), :] = xr_ref[pl.ds(begin, sub), :]
+
+    def relay_middle(e):
+        begin, up, down, sibs = links(e, False)
+        up.wait_recv()
+        send_on(up, down, sibs)
+
+    def relay_last(e):
+        begin, up, down, sibs = links(e, False)
+        up.wait_recv()
+        for sib in sibs:
+            sib.start()
+
+    near = jnp.abs(high - col) == 1
+
+    def between(slot):
+        @pl.when(source)
+        def _():
+            if 2 <= slot + 2 < pieces:
+                relay_source(slot + 2)
+
+        @pl.when(jnp.logical_and(middle, near))
+        def _():
+            if slot == 0:
+                relay_middle(0)
+            if slot + 1 < pieces:
+                relay_middle(slot + 1)
+
+        @pl.when(jnp.logical_and(middle, jnp.logical_not(near)))
+        def _():
+            if 0 <= slot - 1 < pieces:
+                relay_middle(slot - 1)
+
+        @pl.when(last)
+        def _():
+            if 0 <= slot - 2 < pieces:
+                relay_last(slot - 2)
+
+    def owned(h):
+        for copy in t_copies[h * (nc - 1) : (h + 1) * (nc - 1)]:
+            copy.wait()
+        where = pl.ds(pl.multiple_of(col * chunk + h * sub, 8), sub)
+        total = t_ref[where, :]
+        for d in range(1, nc):
+            total = total + tland[d - 1, h * sub : (h + 1) * sub, :]
+        xr_ref[where, :] = total
+
+        @pl.when(source)
+        def _():
+            relay_source(h)
 
     place = 0
     for i in range(size // BLK):
@@ -151,6 +255,8 @@
         spots.append((start, part))
         for copy in copies:
             copy.wait()
+        if level == 1:
+            owned(0)
         mine = acc[pl.ds(start, part), :]
         for d in range(1, n):
             mine = mine + land[pl.ds(slot + (d - 1) * part, part), :]
@@ -167,102 +273,12 @@
             where = full.at[pl.ds(begin, part)]
             copies.append(remote(where, where, base + d - 1, peer(d)))
             copies[-1].start()
+        if level == 1:
+            owned(1)
+            for copy in gathers:
+                copy.start()
         for copy in copies:
             copy.wait()
-
-    gather_base = take(2 * (nc - 1))
-    chain_base = take(pieces)
-    down_base = take(pieces)
-    sib_base = take(pieces * (ratio - 1))
-    gathers = []
-    for d in range(1, nc):
-        for h in range(2):
-            own = xr_ref.at[pl.ds(pl.multiple_of(col * chunk + h * sub, 8), sub)]
-            gathers.append(remote(own, own, gather_base + 2 * (d - 1) + h, col_peer(d)))
-    _, _, low_peer = levels[0]
-    source = high == col
-    top = nc - 1
-    above = (jnp.minimum(high + 1, top) * ratio + low, col)
-    below = (jnp.maximum(high - 1, 0) * ratio + low, col)
-    goes_up = jnp.logical_and(high >= col, high < top)
-    goes_down = jnp.logical_and(high <= col, high > 0)
-    onward = jnp.logical_or(goes_up, goes_down)
-    middle = jnp.logical_and(onward, jnp.logical_not(source))
-    last = jnp.logical_and(jnp.logical_not(onward), jnp.logical_not(source))
-
-    def links(e, src_is_own):
-        begin = pl.multiple_of(lax.rem(col - e // 2 + nc, nc) * chunk + (e % 2) * sub, 8)
-        dst = xc_ref.at[low, pl.ds(begin, sub)]
-        src = xr_ref.at[pl.ds(begin, sub)] if src_is_own else dst
-        up = remote(src, dst, chain_base + e, above)
-        down = pltpu.make_async_remote_copy(
-            src_ref=src, dst_ref=dst, send_sem=send_sem.at[down_base + e],
-            recv_sem=recv_sem.at[chain_base + e], device_id=below, device_id_type=MESH,
-        )
-        sibs = [remote(src, dst, sib_base + e * (ratio - 1) + q - 1, low_peer(q)) for q in range(1, ratio)]
-        return begin, up, down, sibs
-
-    def send_on(up, down, sibs):
-        @pl.when(goes_up)
-        def _():
-            up.start()
-
-        @pl.when(goes_down)
-        def _():
-            down.start()
-
-        for sib in sibs:
-            sib.start()
-
-    def relay_source(e):
-        if e >= 2:
-            gathers[e - 2].wait_recv()
-        begin, up, down, sibs = links(e, True)
-        send_on(up, down, sibs)
-        xc_ref[low, pl.ds(begin, sub), :] = xr_ref[pl.ds(begin, sub), :]
-
-    def relay_middle(e):
-        begin, up, down, sibs = links(e, False)
-        up.wait_recv()
-        send_on(up, down, sibs)
-
-    def relay_last(e):
-        begin, up, down, sibs = links(e, False)
-        up.wait_recv()
-        for sib in sibs:
-            sib.start()
-
-    def between(event):
-        @pl.when(source)
-        def _():
-            if 2 <= event + 1 < pieces:
-                relay_source(event + 1)
-
-        @pl.when(middle)
-        def _():
-            if event < pieces:
-                relay_middle(event)
-
-        @pl.when(last)
-        def _():
-            if 0 <= event - 2 < pieces:
-                relay_last(event - 2)
-
-    for copy in t_copies:
-        copy.wait()
-    where = pl.ds(pl.multiple_of(col * chunk, 8), chunk)
-    owned = t_ref[where, :]
-    for d in range(1, nc):
-        owned = owned + tland[d - 1]
-    xr_ref[where, :] = owned
-
-    @pl.when(source)
-    def _():
-        relay_source(0)
-        relay_source(1)
-
-    for copy in gathers:
-        copy.start()
 
     same = lax.broadcasted_iota(jnp.int32, (BLK, BLK), 0) == lax.broadcasted_iota(jnp.int32, (BLK, BLK), 1)
     for index, (i, j) in enumerate(pair_blocks(size)):
@@ -276,11 +292,10 @@
     tail = len(pair_blocks(size)) * BLK
     pred_ref[...] = full[tail : tail + 8, :]
 
-    events = 2 * (size // BLK)
+    between(0)
     factor_inverse(mat, work, cols, between)
-    inv_ref[...] = mat[:, size:]
-    for event in range(events, pieces + 2):
-        between(event)
+    inverse = mat[:, size:]
+    inv_ref[...] = inverse
     for copy in gathers:
         copy.wait_send()
 
@@ -288,6 +303,14 @@
     def _():
         for copy in gathers:
             copy.wait_recv()
+
+    for slot in range(2 * (size // BLK) + 1, pieces):
+        between(slot)
+    gain_ref[...] = lax.dot_general(
+        xr_ref[...], inverse, (((1,), (1,)), ((), ())), precision=MID, preferred_element_type=jnp.float32
+    )
+    for slot in range(max(pieces, 2 * (size // BLK) + 1), pieces + 2):
+        between(slot)
 
     for e in range(pieces):
         _, up, down, sibs = links(e, False)
@@ -326,6 +349,7 @@
         in_specs=[vmem] * 4,
         out_specs=(vmem,) * 4,
         scratch_shapes=[
+            pltpu.VMEM((rows, size), f32),
             pltpu.VMEM((total, BLK), f32),
             pltpu.VMEM((total, BLK), f32),
             pltpu.VMEM((landing, BLK), f32),
@@ -372,13 +396,12 @@
     filled = len(pair_blocks(total)) * BLK + 8
     unit = 8 * devices
     packed = -(-(filled + 8) // unit) * unit
-    inverse, cross, cross_cols, pred = exchange(mesh, packed, part, row_op, part_pred, variance)
+    inverse, gain, cross_cols, pred = exchange(mesh, packed, part, row_op, part_pred, variance)
     predicted = pred[: total // BLK].reshape(total)
     innov = values - predicted
-    white = dot(inverse, innov[:, None], HI)
-    gain = dot(cross, inverse.T, MID)
+    white = jnp.sum(inverse * innov[None, :], axis=1)
     gain_cols = dot(cross_cols.reshape(cols_dev, total), inverse.T, MID)
-    mean = state_mean + dot(gain, white, HI)[:, 0]
+    mean = state_mean + jnp.sum(gain * white[None, :], axis=1)
     matrix = covariance - dot(gain, gain_cols.T, MID)
     return (matrix, mean)
 

time: 138 us -> 132 us (0.957)
  matrix products: 28.5 us -> 23.9 us
  Pallas kernels: 104 us -> 102 us
    dot_general x6 -> x3, matrix products: 28.5 us -> 23.9 us  [dot(): jnp.dot(a, b, precision=precision, preferred_element_type=jnp.float32)]
where the time goes in v1:
time: 132 us
  Pallas kernels  102 us (77%)
  matrix products  23.9 us (18%)
  local copies, waits for them, and re-layouts  3.11 us (2%)
  other arithmetic  1.96 us (1%)
    pallas_call x1, Pallas kernels, exchange(): pl.pallas_call(functools.partial(kernel, nr, nc), out_shape=(jax.ShapeDty...  102 us
    dot_general x3, matrix products, dot(): jnp.dot(a, b, precision=precision, preferred_element_type=jnp.float32)  23.9 us

profile of v1, /device:TPU:7, one launch (start us, length us, event | category | flops | bytes accessed | tf_op | source)
XLA Modules:
  0.0 132.0 jit_solution(11837667793649230356)
XLA Ops:
  0.6 0.7 copy.11
  1.3 0.7 copy.10
  2.0 0.9 fusion.26
  2.9 0.9 fusion.27
  3.7 0.0 copy-start
  3.7 10.7 %fusion.22.t_ref = f32[1024,512]{1,0:T(8,128)S(1)} fusion(f32[1024,2048]{1,0:T(8,128)} %param.6, f32[512]{0:T(512)S(1)} %bitcast.41, s32[512]{0:T(512)S(1)} %bitcast.33, f32[512]{0:T(512)S(1)} %bitcast.43, s32[512]{0:T(512)S(1)} %bitcast.35, f32[512]{0:T(512)S(1)} %bitcast.45, s32[512]{0:T(512)S(1)} %bitcast.37, f32[512]{0:T(512)S(1)} %bitcast.39, ...), kind=kOutput, calls=%fused_computation.26 | convolution fusion | flops 6453985280 | bytes 10510336 | tf_op jit(solution)/shard_map/dot_general | solution.py:368
  14.4 0.0 copy-done
  14.4 1.0 multiply_reduce_fusion.1
  15.4 0.0 slice-start
  15.4 102.3 %shard_map.77 = (f32[512,512]{1,0:T(8,128)S(1)}, f32[1024,512]{1,0:T(8,128)S(1)}, f32[2,1024,512]{2,1,0:T(8,128)S(1)}, f32[8,128]{1,0:T(8,128)S(1)}) custom-call(f32[1024,512]{1,0:T(8,128)S(1)} %fusion.22.t_ref, f32[1024,512]{1,0:T(8,128)S(1)} %get-tuple-element.11.op_ref, f32[8,128]{1,0:T(8,128)S(1)} %pad.4.part_ref, f32[1,512]{1,0:T(1,128)S(1)} %bitcast.28), custom_call_target="tpu_custom_call" | custom-call | tf_op jit(solution)/shard_map/pallas_call | solution.py:341
  117.8 0.0 slice-start.1
  117.8 3.6 %fusion.28 = f32[2048,512]{1,0:T(8,128)S(1)} fusion(f32[2048,512]{1,0:T(8,128)S(1)} %bitcast.27, f32[512,512]{1,0:T(8,128)S(1)} %get-tuple-element.8), kind=kOutput, calls=%fused_computation.35 | convolution fusion | flops 3221225472 | bytes 9437184 | tf_op jit(solution)/shard_map/dot_general | solution.py:368
  121.5 0.2 multiply_reduce_fusion.2
  121.6 0.2 multiply_reduce_fusion
  121.8 0.6 add.55
  122.4 0.0 slice-done
  122.4 0.0 slice-done.1
  122.4 9.6 %convolution_subtract_fusion = f32[1024,2048]{1,0:T(8,128)} fusion(f32[1024,2048]{1,0:T(8,128)S(1)} %bitcast.30, f32[1024,512]{1,0:T(8,128)S(1)} %get-tuple-element.6, f32[2048,512]{1,0:T(8,128)S(1)} %fusion.28), kind=kOutput, calls=%fused_computation.12 | convolution fusion | flops 6444548096 | bytes 23068672 | tf_op jit(solution)/shard_map/dot_general | solution.py:368
  (6 shorter events, 0.0 us)
Async XLA Ops:
  3.7 10.7 %copy-start = (f32[1024]{0:T(1024)S(1)}, f32[1024]{0:T(1024)}, u32[]{:S(2)}) copy-start(f32[1024]{0:T(1024)} %param.7) | copy-start | bytes 12292
  15.4 107.0 %slice-start = ((s8[8388608]{0:T(1024)(128)(4,1)}), s8[4194304]{0:T(1024)(128)(4,1)S(1)}, s32[]{:S(2)}) async-start(s8[8388608]{0:T(1024)(128)(4,1)} %bitcast.29), calls=%async_computation | async-start | bytes 8388608
  117.8 4.7 %slice-start.1 = ((s8[8388608]{0:T(1024)(128)(4,1)}), s8[4194304]{0:T(1024)(128)(4,1)S(1)}, s32[]{:S(2)}) async-start(s8[8388608]{0:T(1024)(128)(4,1)} %bitcast.29), calls=%async_computation.1 | async-start | bytes 8388608

commit v2 on v1

--- a/solution.py
+++ b/solution.py
@@ -17,8 +17,7 @@
     def panel_step(first, g, carry):
         start = pl.multiple_of(g * SUB, SUB)
         panel = work[pl.ds(start, SUB), :]
-        cols[:, :SUB] = panel[:, :BLK].T
-        square = cols[pl.ds(start, SUB), :SUB]
+        square = pltpu.roll(panel[:, :BLK], BLK - start, 1)[:, :SUB]
         wide = [jnp.broadcast_to(square[:, j : j + 1], (SUB, BLK)) for j in range(SUB)]
         left, right = panel[:, :BLK], panel[:, BLK:]
         below = lax.broadcasted_iota(jnp.int32, (SUB, BLK), 0)
@@ -172,7 +171,7 @@
         if e >= 2:
             gathers[e - 2].wait_recv()
         begin, up, down, sibs = links(e, True)
-        send_on(up, down, sibs)
+        send_on(up, down, sibs if e >= 2 else [])
         xc_ref[low, pl.ds(begin, sub), :] = xr_ref[pl.ds(begin, sub), :]
 
     def relay_middle(e):
@@ -191,6 +190,10 @@
     def between(slot):
         @pl.when(source)
         def _():
+            if slot == 0:
+                for e in range(2):
+                    for sib in links(e, True)[3]:
+                        sib.start()
             if 2 <= slot + 2 < pieces:
                 relay_source(slot + 2)
 
@@ -255,8 +258,6 @@
         spots.append((start, part))
         for copy in copies:
             copy.wait()
-        if level == 1:
-            owned(0)
         mine = acc[pl.ds(start, part), :]
         for d in range(1, n):
             mine = mine + land[pl.ds(slot + (d - 1) * part, part), :]
@@ -279,6 +280,8 @@
                 copy.start()
         for copy in copies:
             copy.wait()
+        if level == 2:
+            owned(0)
 
     same = lax.broadcasted_iota(jnp.int32, (BLK, BLK), 0) == lax.broadcasted_iota(jnp.int32, (BLK, BLK), 1)
     for index, (i, j) in enumerate(pair_blocks(size)):

time: 132 us -> 131 us (level)
  Pallas kernels: 102 us -> 100 us
    pallas_call x1, Pallas kernels: 102 us -> 100 us  [exchange(): pl.pallas_call(functools.partial(kernel, nr, nc), out_shape=(jax.ShapeDty...]
where the time goes in v2:
time: 131 us; the launch traced here: 130 us
  Pallas kernels  100 us (76%)
  matrix products  23.9 us (18%)
  local copies, waits for them, and re-layouts  3.11 us (2%)
  other arithmetic  1.96 us (1%)
    pallas_call x1, Pallas kernels, exchange(): pl.pallas_call(functools.partial(kernel, nr, nc), out_shape=(jax.ShapeDty...  100 us
    dot_general x3, matrix products, dot(): jnp.dot(a, b, precision=precision, preferred_element_type=jnp.float32)  23.9 us

profile of v2, /device:TPU:7, one launch (start us, length us, event | category | flops | bytes accessed | tf_op | source)
XLA Modules:
  0.0 129.8 jit_solution(8134509753465996168)
XLA Ops:
  0.6 0.7 copy.11
  1.3 0.7 copy.10
  2.0 0.9 fusion.26
  2.9 0.9 fusion.27
  3.7 0.0 copy-start
  3.7 10.7 %fusion.22.t_ref = f32[1024,512]{1,0:T(8,128)S(1)} fusion(f32[1024,2048]{1,0:T(8,128)} %param.6, f32[512]{0:T(512)S(1)} %bitcast.41, s32[512]{0:T(512)S(1)} %bitcast.33, f32[512]{0:T(512)S(1)} %bitcast.43, s32[512]{0:T(512)S(1)} %bitcast.35, f32[512]{0:T(512)S(1)} %bitcast.45, s32[512]{0:T(512)S(1)} %bitcast.37, f32[512]{0:T(512)S(1)} %bitcast.39, ...), kind=kOutput, calls=%fused_computation.26 | convolution fusion | flops 6453985280 | bytes 10510336 | tf_op jit(solution)/shard_map/dot_general | solution.py:371
  14.4 0.0 copy-done
  14.4 1.0 multiply_reduce_fusion.1
  15.4 0.0 slice-start
  15.4 100.1 %shard_map.77 = (f32[512,512]{1,0:T(8,128)S(1)}, f32[1024,512]{1,0:T(8,128)S(1)}, f32[2,1024,512]{2,1,0:T(8,128)S(1)}, f32[8,128]{1,0:T(8,128)S(1)}) custom-call(f32[1024,512]{1,0:T(8,128)S(1)} %fusion.22.t_ref, f32[1024,512]{1,0:T(8,128)S(1)} %get-tuple-element.11.op_ref, f32[8,128]{1,0:T(8,128)S(1)} %pad.4.part_ref, f32[1,512]{1,0:T(1,128)S(1)} %bitcast.28), custom_call_target="tpu_custom_call" | custom-call | tf_op jit(solution)/shard_map/pallas_call | solution.py:344
  115.5 0.0 slice-start.1
  115.6 3.6 %fusion.28 = f32[2048,512]{1,0:T(8,128)S(1)} fusion(f32[2048,512]{1,0:T(8,128)S(1)} %bitcast.27, f32[512,512]{1,0:T(8,128)S(1)} %get-tuple-element.8), kind=kOutput, calls=%fused_computation.35 | convolution fusion | flops 3221225472 | bytes 9437184 | tf_op jit(solution)/shard_map/dot_general | solution.py:371
  119.2 0.2 multiply_reduce_fusion.2
  119.4 0.2 multiply_reduce_fusion
  119.6 0.6 add.55
  120.2 0.0 slice-done
  120.2 0.0 slice-done.1
  120.2 9.6 %convolution_subtract_fusion = f32[1024,2048]{1,0:T(8,128)} fusion(f32[1024,2048]{1,0:T(8,128)S(1)} %bitcast.30, f32[1024,512]{1,0:T(8,128)S(1)} %get-tuple-element.6, f32[2048,512]{1,0:T(8,128)S(1)} %fusion.28), kind=kOutput, calls=%fused_computation.12 | convolution fusion | flops 6444548096 | bytes 23068672 | tf_op jit(solution)/shard_map/dot_general | solution.py:371
  (6 shorter events, 0.0 us)
Async XLA Ops:
  3.7 10.7 %copy-start = (f32[1024]{0:T(1024)S(1)}, f32[1024]{0:T(1024)}, u32[]{:S(2)}) copy-start(f32[1024]{0:T(1024)} %param.7) | copy-start | bytes 12292
  15.4 104.8 %slice-start = ((s8[8388608]{0:T(1024)(128)(4,1)}), s8[4194304]{0:T(1024)(128)(4,1)S(1)}, s32[]{:S(2)}) async-start(s8[8388608]{0:T(1024)(128)(4,1)} %bitcast.29), calls=%async_computation | async-start | bytes 8388608
  115.5 4.7 %slice-start.1 = ((s8[8388608]{0:T(1024)(128)(4,1)}), s8[4194304]{0:T(1024)(128)(4,1)S(1)}, s32[]{:S(2)}) async-start(s8[8388608]{0:T(1024)(128)(4,1)} %bitcast.29), calls=%async_computation.1 | async-start | bytes 8388608

commit v3 on v2

--- a/solution.py
+++ b/solution.py
@@ -194,8 +194,9 @@
                 for e in range(2):
                     for sib in links(e, True)[3]:
                         sib.start()
-            if 2 <= slot + 2 < pieces:
-                relay_source(slot + 2)
+                relay_source(2)
+            if slot + 3 < pieces:
+                relay_source(slot + 3)
 
         @pl.when(jnp.logical_and(middle, near))
         def _():
@@ -206,8 +207,10 @@
 
         @pl.when(jnp.logical_and(middle, jnp.logical_not(near)))
         def _():
-            if 0 <= slot - 1 < pieces:
+            if 0 <= slot - 1 < pieces - 1:
                 relay_middle(slot - 1)
+            if slot == pieces - 1:
+                relay_middle(pieces - 1)
 
         @pl.when(last)
         def _():

time: 131 us -> 131 us (level)
  no operation moved by 1% of the time
where the time goes in v3:
time: 131 us; the launch traced here: 130 us
  Pallas kernels  100 us (76%)
  matrix products  23.9 us (18%)
  local copies, waits for them, and re-layouts  3.11 us (2%)
  other arithmetic  1.96 us (1%)
    pallas_call x1, Pallas kernels, exchange(): pl.pallas_call(functools.partial(kernel, nr, nc), out_shape=(jax.ShapeDty...  100 us
    dot_general x3, matrix products, dot(): jnp.dot(a, b, precision=precision, preferred_element_type=jnp.float32)  23.9 us

profile of v3, /device:TPU:7, one launch (start us, length us, event | category | flops | bytes accessed | tf_op | source)
XLA Modules:
  0.0 129.8 jit_solution(9097348607479517674)
XLA Ops:
  0.6 0.7 copy.11
  1.3 0.7 copy.10
  2.0 0.9 fusion.26
  2.9 0.9 fusion.27
  3.7 0.0 copy-start
  3.7 10.7 %fusion.22.t_ref = f32[1024,512]{1,0:T(8,128)S(1)} fusion(f32[1024,2048]{1,0:T(8,128)} %param.6, f32[512]{0:T(512)S(1)} %bitcast.41, s32[512]{0:T(512)S(1)} %bitcast.33, f32[512]{0:T(512)S(1)} %bitcast.43, s32[512]{0:T(512)S(1)} %bitcast.35, f32[512]{0:T(512)S(1)} %bitcast.45, s32[512]{0:T(512)S(1)} %bitcast.37, f32[512]{0:T(512)S(1)} %bitcast.39, ...), kind=kOutput, calls=%fused_computation.26 | convolution fusion | flops 6453985280 | bytes 10510336 | tf_op jit(solution)/shard_map/dot_general | solution.py:374
  14.4 0.0 copy-done
  14.4 1.0 multiply_reduce_fusion.1
  15.4 0.0 slice-start
  15.4 100.1 %shard_map.77 = (f32[512,512]{1,0:T(8,128)S(1)}, f32[1024,512]{1,0:T(8,128)S(1)}, f32[2,1024,512]{2,1,0:T(8,128)S(1)}, f32[8,128]{1,0:T(8,128)S(1)}) custom-call(f32[1024,512]{1,0:T(8,128)S(1)} %fusion.22.t_ref, f32[1024,512]{1,0:T(8,128)S(1)} %get-tuple-element.11.op_ref, f32[8,128]{1,0:T(8,128)S(1)} %pad.4.part_ref, f32[1,512]{1,0:T(1,128)S(1)} %bitcast.28), custom_call_target="tpu_custom_call" | custom-call | tf_op jit(solution)/shard_map/pallas_call | solution.py:347
  115.5 0.0 slice-start.1
  115.6 3.6 %fusion.28 = f32[2048,512]{1,0:T(8,128)S(1)} fusion(f32[2048,512]{1,0:T(8,128)S(1)} %bitcast.27, f32[512,512]{1,0:T(8,128)S(1)} %get-tuple-element.8), kind=kOutput, calls=%fused_computation.35 | convolution fusion | flops 3221225472 | bytes 9437184 | tf_op jit(solution)/shard_map/dot_general | solution.py:374
  119.2 0.2 multiply_reduce_fusion.2
  119.4 0.2 multiply_reduce_fusion
  119.6 0.6 add.55
  120.2 0.0 slice-done
  120.2 0.0 slice-done.1
  120.2 9.6 %convolution_subtract_fusion = f32[1024,2048]{1,0:T(8,128)} fusion(f32[1024,2048]{1,0:T(8,128)S(1)} %bitcast.30, f32[1024,512]{1,0:T(8,128)S(1)} %get-tuple-element.6, f32[2048,512]{1,0:T(8,128)S(1)} %fusion.28), kind=kOutput, calls=%fused_computation.12 | convolution fusion | flops 6444548096 | bytes 23068672 | tf_op jit(solution)/shard_map/dot_general | solution.py:374
  (6 shorter events, 0.0 us)
Async XLA Ops:
  3.7 10.7 %copy-start = (f32[1024]{0:T(1024)S(1)}, f32[1024]{0:T(1024)}, u32[]{:S(2)}) copy-start(f32[1024]{0:T(1024)} %param.7) | copy-start | bytes 12292
  15.4 104.8 %slice-start = ((s8[8388608]{0:T(1024)(128)(4,1)}), s8[4194304]{0:T(1024)(128)(4,1)S(1)}, s32[]{:S(2)}) async-start(s8[8388608]{0:T(1024)(128)(4,1)} %bitcast.29), calls=%async_computation | async-start | bytes 8388608
  115.5 4.7 %slice-start.1 = ((s8[8388608]{0:T(1024)(128)(4,1)}), s8[4194304]{0:T(1024)(128)(4,1)S(1)}, s32[]{:S(2)}) async-start(s8[8388608]{0:T(1024)(128)(4,1)} %bitcast.29), calls=%async_computation.1 | async-start | bytes 8388608
